TPU v7x, 32 devices: a whole 2x2x4 slice. The times are simulated.
32 devices in a mesh: groups: 2 (over y), row: 16 (over z, x, core).
Axes of the slice: x: 2, y: 2, z: 4, core: 2. Of those that a mesh axis runs over, the one named last changes fastest.
Arguments:
- object_tiles: bfloat16 [8192, 2, 2048], P(('groups', 'row')), parts along dimension 0, may hold values from -4 to 4
- probe: float32 [4, 256, 2, 256], replicated, may hold values from -3 to 3
- measured: bfloat16 [192, 256, 256], P(('groups', 'row')), parts along dimension 0, may hold values from 0.19921875 to 2.5
- offset_row: int32 [192], P(('groups', 'row')), parts along dimension 0, may hold values from 0 to 255
- offset_col: int32 [192], P(('groups', 'row')), parts along dimension 0, may hold values from 0 to 1791
- subpixel: int32 [192], P(('groups', 'row')), parts along dimension 0, may hold values from 0 to 15
- live_count: int32 [32], P(('groups', 'row')), parts along dimension 0, may hold values from 1 to 6, 48 in all
Outputs:
- object_grad: float32 [8192, 2, 2048], P(('groups', 'row')), parts along dimension 0
- probe_grad: float32 [8, 256, 2, 256], P('groups'), parts along dimension 0
- position_grad: float32 [2, 192], P(None, ('groups', 'row')), parts along dimension 1
There are 2 independent parts, one for each index of `groups`. A program takes and returns all parts, laid end to end along the dimension named above; an argument that names none is the same for every part. Nothing has to cross between parts.
Inputs may be any that keep to these rules, and one draw needn't show every extreme that they name: Device d's live slots are its first live_count[d] slots; live_count sums to 48 and reaches 6 on some device.
All inputs are finite; a program needn't handle non-finite values.
Results may differ from a plain program's by a relative error of at most 0.0099.
Values may be sent and summed in bfloat16 or wider, within the bound.
A program may use at most 128 MiB of HBM per device.

v0:
```python
import math
import jax
import jax.numpy as jnp
from jax import lax
from jax.sharding import PartitionSpec as P


def passed_along(x, axis, by):
    length = lax.axis_size(axis)
    pairs = [(i, i + by) for i in range(length) if 0 <= i + by < length]
    return lax.ppermute(x, axis, pairs)


def dft_tables(patch):
    index = jnp.arange(patch, dtype=jnp.int32)
    phase = index[:, None] * index[None, :] % patch
    angle = phase.astype(jnp.float32) * (2.0 * math.pi / patch)
    scale = 1.0 / math.sqrt(patch)
    cosine = (jnp.cos(angle) * scale).astype(jnp.bfloat16)
    sine = (jnp.sin(angle) * scale).astype(jnp.bfloat16)
    along_x = jnp.concatenate(
        [jnp.concatenate([cosine, -sine], 1), jnp.concatenate([sine, cosine], 1)], 0
    )
    along_y = jnp.concatenate(
        [
            jnp.stack([cosine, sine], -1).reshape(patch, 2 * patch),
            jnp.stack([-sine, cosine], -1).reshape(patch, 2 * patch),
        ],
        0,
    )
    inverse_y = jnp.stack(
        [jnp.concatenate([cosine, -sine], 1), jnp.concatenate([sine, cosine], 1)], 1
    ).reshape(2 * patch, 2 * patch)
    inverse_x = jnp.concatenate(
        [jnp.concatenate([cosine, sine], 1), jnp.concatenate([-sine, cosine], 1)], 0
    )
    return (along_x, along_y, inverse_y, inverse_x)


def fractions(code):
    return ((code // 4).astype(jnp.float32) * 0.25, (code % 4).astype(jnp.float32) * 0.25)


def interpolate(window, code):
    frac_y, frac_x = fractions(code)
    cells = window.astype(jnp.float32)
    size = cells.shape[0] - 1
    upper = (1.0 - frac_x) * cells[:size, :, :size] + frac_x * cells[:size, :, 1:]
    lower = (1.0 - frac_x) * cells[1:, :, :size] + frac_x * cells[1:, :, 1:]
    return (1.0 - frac_y) * upper + frac_y * lower


def spread(grad_patch, frac_y, frac_x):

    def sideways(part):
        return jnp.pad((1.0 - frac_x) * part, ((0, 0), (0, 0), (0, 1))) + jnp.pad(
            frac_x * part, ((0, 0), (0, 0), (1, 0))
        )

    upper = sideways((1.0 - frac_y) * grad_patch)
    lower = sideways(frac_y * grad_patch)
    return jnp.pad(upper, ((0, 1), (0, 0), (0, 0))) + jnp.pad(lower, ((1, 0), (0, 0), (0, 0)))


def slopes(window, grad_patch, frac_y, frac_x):
    cells = window.astype(jnp.float32)
    size = cells.shape[0] - 1
    down = cells[1:] - cells[:size]
    slope_y = (1.0 - frac_x) * down[:, :, :size] + frac_x * down[:, :, 1:]
    across = cells[:, :, 1:] - cells[:, :, :size]
    slope_x = (1.0 - frac_y) * across[:size] + frac_y * across[1:]
    return (jnp.sum(grad_patch * slope_y) / size, jnp.sum(grad_patch * slope_x) / size)


def project(patch_obj, amplitude, probe, tables):
    along_x, along_y, inverse_y, inverse_x = tables
    modes = probe.shape[0]
    size = probe.shape[1]
    preal = probe[:, :, 0, :]
    pimag = probe[:, :, 1, :]
    oreal = patch_obj[:, 0, :]
    oimag = patch_obj[:, 1, :]
    wave = jnp.stack([preal * oreal - pimag * oimag, preal * oimag + pimag * oreal], axis=2).astype(
        jnp.bfloat16
    )
    first = jnp.dot(
        wave.reshape(modes * size, 2 * size), along_x, preferred_element_type=jnp.float32
    ).astype(jnp.bfloat16)
    far = jnp.einsum(
        "ab,mbk->mak",
        along_y,
        first.reshape(modes, 2 * size, size),
        preferred_element_type=jnp.float32,
    )
    far = far.reshape(modes, 2, size, size)
    modulus = jnp.maximum(jnp.sqrt(jnp.sum(far * far, axis=(0, 1))), 0.5)
    ratio = 1.0 - amplitude.astype(jnp.float32) / modulus
    error = (far * ratio).astype(jnp.bfloat16)
    back = jnp.einsum(
        "ab,mbk->mak",
        inverse_y,
        error.reshape(modes, 2 * size, size),
        preferred_element_type=jnp.float32,
    ).astype(jnp.bfloat16)
    exit_grad = jnp.dot(
        back.reshape(modes * size, 2 * size), inverse_x, preferred_element_type=jnp.float32
    ).reshape(modes, size, 2, size)
    ureal = exit_grad[:, :, 0, :]
    uimag = exit_grad[:, :, 1, :]
    obj_grad = jnp.stack(
        [jnp.sum(preal * ureal + pimag * uimag, 0), jnp.sum(preal * uimag - pimag * ureal, 0)],
        axis=1,
    )
    probe_term = jnp.stack([oreal * ureal + oimag * uimag, oreal * uimag - oimag * ureal], axis=2)
    return (obj_grad, probe_term)


def shards(object_tiles, probe, measured, offset_row, offset_col, subpixel, live_count):
    rows = object_tiles.shape[0]
    width = object_tiles.shape[2]
    size = probe.shape[1]
    slots = measured.shape[0]
    spare = slots // 2
    tables = dft_tables(size)
    count = live_count[0]
    slot_ids = jnp.arange(slots, dtype=jnp.int32)
    rim = passed_along(object_tiles, "row", -1)
    extended = jnp.concatenate([object_tiles, rim], axis=0)

    def cut(index):
        return lax.dynamic_slice(
            extended, (offset_row[index], 0, offset_col[index]), (size + 1, 2, size + 1)
        )

    windows = lax.map(cut, slot_ids)
    empty_grads = jnp.zeros((slots + spare, size, 2, size), jnp.float32)
    empty_probe = jnp.zeros(probe.shape, jnp.float32)

    def own_slot(index, carry):
        grads, probe_acc = carry
        patch_obj = interpolate(windows[index], subpixel[index])
        obj_grad, probe_term = project(patch_obj, measured[index], probe, tables)
        return (grads.at[index].set(obj_grad), probe_acc + probe_term)

    grads, probe_acc = lax.fori_loop(0, count, own_slot, (empty_grads, empty_probe))
    probe_grad = lax.psum(probe_acc, "row")

    def settle(index, carry):
        grad_ext, moved = carry
        frac_y, frac_x = fractions(subpixel[index])
        obj_grad = grads[index]
        corner = (offset_row[index], 0, offset_col[index])
        region = lax.dynamic_slice(grad_ext, corner, (size + 1, 2, size + 1))
        grad_ext = lax.dynamic_update_slice(
            grad_ext, region + spread(obj_grad, frac_y, frac_x), corner
        )
        slope_y, slope_x = slopes(windows[index], obj_grad, frac_y, frac_x)
        moved = moved.at[:, index].set(jnp.stack([slope_y, slope_x]))
        return (grad_ext, moved)

    start = (jnp.zeros((rows + size, 2, width), jnp.float32), jnp.zeros((2, slots), jnp.float32))
    grad_ext, moved = lax.fori_loop(0, count, settle, start)
    own_rows = grad_ext[:rows]
    below = passed_along(grad_ext[rows:], "row", 1)
    object_grad = own_rows.at[:size].add(below)
    return (object_grad, probe_grad, moved)


def solution(mesh):
    in_specs = (
        P(("groups", "row"), None, None),
        P(),
        P(("groups", "row"), None, None),
        P(("groups", "row")),
        P(("groups", "row")),
        P(("groups", "row")),
        P(("groups", "row")),
    )
    out_specs = (
        P(("groups", "row"), None, None),
        P("groups", None, None, None),
        P(None, ("groups", "row")),
    )
    return jax.shard_map(shards, mesh=mesh, in_specs=in_specs, out_specs=out_specs, check_vma=False)
```

profile of v0, /device:TPU:0, one launch (start us, length us, event | category | flops | bytes accessed | tf_op | source)
XLA Modules:
  0.0 838.3 jit_solution(12319592840080099803)
XLA Ops:
  16.4 1.8 copy.45
  18.2 9.6 %pad_maximum_fusion.1 = bf16[512,2,2048]{2,1,0:T(2,128)(2,1)} fusion(bf16[256,2,2048]{2,1,0:T(2,128)(2,1)} %collective-permute-done, bf16[256,2,2048]{2,1,0:T(2,128)(2,1)} %param.21), kind=kLoop, calls=%fused_computation.72 | loop fusion | flops 2097152 | bytes 8388608 | tf_op jit(solution)/shard_map/concatenate | solution.py:128
  27.8 56.9 %while.42 = (s32[]{:T(128)}, bf16[6,257,2,257]{3,2,1,0:T(2,128)(2,1)}, s32[6]{0:T(128)S(1)}, s32[6]{0:T(128)S(1)}, s32[6]{0:T(128)S(1)}, /*index=5*/bf16[512,2,2...) while((s32[]{:T(128)}, bf16[6,257,2,257]{3,2,1,0:T(2,128)(2,1)}, ...), condition=%wide.region_1.2_spmd, body=%wide.region_0.1_spmd.sunk | while | flops 11 | bytes 789771 | solution.py:135
  34.6 2.6 bitcast_dynamic-update-slice_fusion.2
  44.1 2.6 bitcast_dynamic-update-slice_fusion.2
  53.5 2.6 bitcast_dynamic-update-slice_fusion.2
  62.9 2.6 bitcast_dynamic-update-slice_fusion.2
  72.2 2.6 bitcast_dynamic-update-slice_fusion.2
  81.7 2.6 bitcast_dynamic-update-slice_fusion.2
  84.7 1.5 broadcast_in_dim.23
  86.2 3.6 broadcast_in_dim.22
  89.9 32.7 %while.43 = (s32[]{:T(128)}, f32[9,256,2,256]{3,2,1,0:T(2,128)}, f32[4,256,2,256]{3,1,2,0:T(8,128)}, s32[]{:T(128)}, f32[4,256,2,256]{3,1,2,0:T(8,128)S(1)}, /*i...) while((s32[]{:T(128)}, f32[9,256,2,256]{3,2,1,0:T(2,128)}, ...), condition=%wide.region_8.9_spmd, body=%wide.region_2.8_spmd.sunk | while | flops 2159608832 | bytes 92680056 | solution.py:145
  99.5 1.7 convolution_convert_fusion.3
  101.1 1.4 reshape.293
  102.6 4.0 fusion.77
  110.1 1.8 fusion.79
  113.2 1.4 reshape.294
  114.7 1.8 fusion.80
  118.6 3.1 fusion.81
  122.6 7.5 broadcast_in_dim.21
  130.2 68.5 %while.44 = (s32[]{:T(128)}, f32[512,2,2048]{2,1,0:T(2,128)}, f32[2,6]{0,1:T(8,128)S(1)}, s32[]{:T(128)}, s32[6]{0:T(128)S(1)}, /*index=5*/s32[6]{0:T(128)S(1)},...) while((s32[]{:T(128)}, f32[512,2,2048]{2,1,0:T(2,128)}, ...), condition=%wide.region_13.14_spmd, body=%wide.region_9.13_spmd.sunk | while | flops 3019835 | bytes 15514405 | solution.py:162
  139.5 1.4 fusion.82
  141.8 3.0 fusion.84
  146.6 1.7 pad_add_fusion.3
  148.3 2.2 add_add_fusion.2
  150.5 47.5 %dynamic_update_slice.14 = f32[512,2,2048]{2,1,0:T(2,128)} dynamic-update-slice(f32[512,2,2048]{2,1,0:T(2,128)} %get-tuple-element.846, f32[257,2,257]{2,1,0:T(2,128)S(1)} %add_add_fusion.2, s32[]{:T(128)S(6)} %select_n.184, s32[]{:T(128)} %constant.305.clone.1..sunk.2, s32[]{:T(128)S(6)} %select_n.185) | dynamic-update-slice | bytes 1056788 | tf_op jit(solution)/shard_map/while/body/dynamic_update_slice | solution.py:154
  198.7 6.3 slice.174
  204.9 321.3 %collective-permute-start.1 = (f32[256,2,2048]{2,1,0:T(2,128)}, f32[256,2,2048]{2,1,0:T(2,128)}, u32[]{:S(2)}, u32[]{:S(2)}) collective-permute-start(f32[256,2,2048]{2,1,0:T(2,128)} %slice.174), channel_id=1, source_target_pairs={{0,1},{1,2},{2,3},{3,4},{4,5},{5,6},{6,7},{7,8},{8,9},{9,10},{10,1... | collective-permute-start | bytes 12582920 | tf_op jit(solution)/shard_map/ppermute | solution.py:11
  526.3 2.9 copy.50
  531.2 9.5 %slice_add_fusion = f32[256,2,2048]{2,1,0:T(2,128)} fusion(f32[256,2,2048]{2,1,0:T(2,128)} %collective-permute-done.1, f32[512,2,2048]{2,1,0:T(2,128)} %get-tuple-element.358), kind=kLoop, calls=%fused_computation.73 | loop fusion | flops 1048576 | bytes 12582912 | tf_op jit(solution)/shard_map/add | solution.py:165
  540.7 287.0 %all-reduce.8.cloned.1.call-done = f32[4,256,2,256]{3,2,1,0:T(2,128)} async-done(((f32[4,256,2,256]{3,2,1,0:T(2,128)}), f32[4,256,2,256]{3,2,1,0:T(2,128)}) %all-reduce.8.cloned.1.call-update) | async-done | bytes 2097168 | tf_op jit(solution)/shard_map/psum | solution.py:146
  827.6 3.6 copy.102
  (102 shorter events, 38.7 us)
Async XLA Ops:
  7.2 820.5 %all-reduce.8.cloned.1.call-start = ((), (), s32[]{:S(2)}) async-start(), calls=%async_computation | async-start | bytes 4194304 | tf_op jit(solution)/shard_map/psum | solution.py:146
  7.2 11.0 %collective-permute-start = (bf16[256,2,2048]{2,1,0:T(2,128)(2,1)}, bf16[256,2,2048]{2,1,0:T(2,128)(2,1)}, u32[]{:S(2)}, u32[]{:S(2)}) collective-permute-start(bf16[256,2,2048]{2,1,0:T(2,128)(2,1)} %param.21), channel_id=1, source_target_pairs={{1,0},{2,1},{3,2},{4,3},{5,4},{6,5},{7,6},{8,7},{9,8},{10,9},{11,1... | collective-permute-start | bytes 6291464 | tf_op jit(solution)/shard_map/ppermute | solution.py:11
  18.1 9.7 %copy-start.11 = (s32[6]{0:T(128)S(1)}, s32[6]{0:T(128)}, u32[]{:S(2)}) copy-start(s32[6]{0:T(128)} %param.24) | copy-start | bytes 76
  18.2 9.7 %copy-start.12 = (s32[6]{0:T(128)S(1)}, s32[6]{0:T(128)}, u32[]{:S(2)}) copy-start(s32[6]{0:T(128)} %param.25) | copy-start | bytes 76
  86.2 3.7 copy-start.10
  86.2 3.7 copy-start.13
  90.5 6.5 copy-start.6
  90.6 8.9 %copy-start.8 = (bf16[512,512]{1,0:T(8,128)(2,1)}, bf16[512,512]{1,0:T(8,128)(2,1)S(1)}, u32[]{:S(2)}) copy-start(bf16[512,512]{1,0:T(8,128)(2,1)S(1)} %get-tuple-element.804) | copy-start | bytes 1572868 | tf_op jit(solution)/shard_map/while
  97.4 0.7 copy-start.4
  108.5 1.6 copy-start
  114.7 1.8 copy-start.5
  116.5 1.6 copy-start.1
  118.1 3.7 copy-start.7
  118.1 3.7 copy-start.9
  118.6 3.2 copy-start.2
  198.7 327.6 %copy-start.3 = (f32[4,256,2,256]{3,1,2,0:T(8,128)S(1)}, f32[4,256,2,256]{3,1,2,0:T(8,128)}, u32[]{:S(2)}) copy-start(f32[4,256,2,256]{3,1,2,0:T(8,128)} %get-tuple-element.359) | copy-start | bytes 6291460
  204.9 326.3 %collective-permute-start.1 = (f32[256,2,2048]{2,1,0:T(2,128)}, f32[256,2,2048]{2,1,0:T(2,128)}, u32[]{:S(2)}, u32[]{:S(2)}) collective-permute-start(f32[256,2,2048]{2,1,0:T(2,128)} %slice.174), channel_id=1, source_target_pairs={{0,1},{1,2},{2,3},{3,4},{4,5},{5,6},{6,7},{7,8},{8,9},{9,10},{10,1... | collective-permute-start | bytes 12582920 | tf_op jit(solution)/shard_map/ppermute | solution.py:11
Sparse Core Ops, SparseCore 0:
  529.4 298.2 all-reduce.7
where the time goes:
time: 853 us; the launch traced here: 838 us
  starting transfers between devices  323 us (38%)
  waiting for transfers between devices  288 us (34%)
  local copies, waits for them, and re-layouts  119 us (14%)
  loops' own time  43.8 us (5%)
  other arithmetic  40.6 us (5%)
  between operations  14.5 us (2%)
  matrix products  9.26 us (1%)
    ppermute x2, starting transfers between devices, passed_along(): return lax.ppermute(x, axis, pairs)  323 us
    psum x1, waiting for transfers between devices, shards(): probe_grad = lax.psum(probe_acc, 'row')  287 us
    dynamic_update_slice x1, local copies, waits for them, and re-layouts, settle(): lax.dynamic_update_slice(grad_ext, region + spread(obj_grad, frac_y, frac...  47.5 us
    another operation x1, loops' own time, shards(): windows = lax.map(cut, slot_ids)  30.8 us
  transfers between devices with their start and end apart: 3, of which 2 were waited for; matrix products, arithmetic and copies ran while one was open for 3% of the time, Pallas kernels for 0%

commit v1 on v0

--- a/solution.py
+++ b/solution.py
@@ -143,7 +143,7 @@
         return (grads.at[index].set(obj_grad), probe_acc + probe_term)
 
     grads, probe_acc = lax.fori_loop(0, count, own_slot, (empty_grads, empty_probe))
-    probe_grad = lax.psum(probe_acc, "row")
+    probe_grad = jnp.sum(lax.all_gather(probe_acc, "row"), axis=0)
 
     def settle(index, carry):
         grad_ext, moved = carry

time: 853 us -> 837 us (0.981)
  the two profiles are of different devices: /device:TPU:0 before, /device:TPU:24 now
where the time goes in v1:
time: 837 us; the launch traced here: 822 us
  waiting for transfers between devices  469 us (56%)
  local copies, waits for them, and re-layouts  118 us (14%)
  starting transfers between devices  109 us (13%)
  other arithmetic  53.4 us (6%)
  loops' own time  48.3 us (6%)
  between operations  14.4 us (2%)
  matrix products  10.3 us (1%)
    ppermute x2, waiting for transfers between devices, passed_along(): return lax.ppermute(x, axis, pairs)  469 us
    ppermute x2, starting transfers between devices, passed_along(): return lax.ppermute(x, axis, pairs)  108 us
    dynamic_update_slice x1, local copies, waits for them, and re-layouts, settle(): lax.dynamic_update_slice(grad_ext, region + spread(obj_grad, frac_y, frac...  47.5 us
    another operation x1, loops' own time, shards(): windows = lax.map(cut, slot_ids)  35.4 us
  transfers between devices with their start and end apart: 3, of which 2 were waited for; matrix products, arithmetic and copies ran while one was open for 12% of the time, Pallas kernels for 0%

profile of v1, /device:TPU:24, one launch (start us, length us, event | category | flops | bytes accessed | tf_op | source)
XLA Modules:
  0.0 821.6 jit_solution(7800901032170313695)
XLA Ops:
  7.2 2.7 collective-permute-start
  19.4 1.8 copy.43
  21.2 12.6 %collective-permute-done = bf16[256,2,2048]{2,1,0:T(2,128)(2,1)} collective-permute-done((bf16[256,2,2048]{2,1,0:T(2,128)(2,1)}, bf16[256,2,2048]{2,1,0:T(2,128)(2,1)}, u32[]{:S(2)}, u32[]{:S(2)}) %collective-permute-start) | collective-permute-done | bytes 2097184 | tf_op jit(solution)/shard_map/ppermute | solution.py:11
  33.8 9.6 %pad_maximum_fusion.1 = bf16[512,2,2048]{2,1,0:T(2,128)(2,1)} fusion(bf16[256,2,2048]{2,1,0:T(2,128)(2,1)} %collective-permute-done, bf16[256,2,2048]{2,1,0:T(2,128)(2,1)} %param.21), kind=kLoop, calls=%fused_computation.72 | loop fusion | flops 2097152 | bytes 8388608 | tf_op jit(solution)/shard_map/concatenate | solution.py:128
  43.4 61.7 %while.42 = (s32[]{:T(128)}, bf16[6,257,2,257]{3,2,1,0:T(2,128)(2,1)}, s32[6]{0:T(128)S(1)}, s32[6]{0:T(128)S(1)}, s32[6]{0:T(128)S(1)}, /*index=5*/bf16[512,2,2...) while((s32[]{:T(128)}, bf16[6,257,2,257]{3,2,1,0:T(2,128)(2,1)}, ...), condition=%wide.region_1.2_spmd, body=%wide.region_0.1_spmd.sunk | while | flops 11 | bytes 790271 | solution.py:135
  51.0 2.6 bitcast_dynamic-update-slice_fusion.2
  61.3 2.6 bitcast_dynamic-update-slice_fusion.2
  71.4 2.6 bitcast_dynamic-update-slice_fusion.2
  81.6 2.6 bitcast_dynamic-update-slice_fusion.2
  91.9 2.7 bitcast_dynamic-update-slice_fusion.2
  102.1 2.6 bitcast_dynamic-update-slice_fusion.2
  105.2 3.6 broadcast_in_dim.22
  108.8 1.5 broadcast_in_dim.23
  110.3 35.1 %while.43 = (s32[]{:T(128)}, f32[9,256,2,256]{3,2,1,0:T(2,128)}, f32[4,256,2,256]{3,1,2,0:T(8,128)}, s32[]{:T(128)}, f32[4,256,2,256]{3,1,2,0:T(8,128)S(1)}, /*i...) while((s32[]{:T(128)}, f32[9,256,2,256]{3,2,1,0:T(2,128)}, ...), condition=%wide.region_8.9_spmd, body=%wide.region_2.8_spmd.sunk | while | flops 2159608832 | bytes 84291320 | solution.py:145
  117.9 2.7 convolution_convert_fusion.3
  120.6 1.4 reshape.294
  122.1 3.9 fusion.77
  130.6 1.8 fusion.79
  135.2 1.8 fusion.80
  141.5 3.1 fusion.81
  145.5 7.5 broadcast_in_dim.21
  152.9 68.5 %while.44 = (s32[]{:T(128)}, f32[512,2,2048]{2,1,0:T(2,128)}, f32[2,6]{0,1:T(8,128)S(1)}, s32[]{:T(128)}, s32[6]{0:T(128)S(1)}, /*index=5*/s32[6]{0:T(128)S(1)},...) while((s32[]{:T(128)}, f32[512,2,2048]{2,1,0:T(2,128)}, ...), condition=%wide.region_13.14_spmd, body=%wide.region_9.13_spmd.sunk | while | flops 3019835 | bytes 15514397 | solution.py:162
  158.9 3.1 fusion.84
  162.0 1.7 pad_add_fusion.3
  168.5 2.1 add_add_fusion.2
  170.6 47.5 %dynamic_update_slice.14 = f32[512,2,2048]{2,1,0:T(2,128)} dynamic-update-slice(f32[512,2,2048]{2,1,0:T(2,128)} %get-tuple-element.846, f32[257,2,257]{2,1,0:T(2,128)S(1)} %add_add_fusion.2, s32[]{:T(128)S(6)} %select_n.184, s32[]{:T(128)} %constant.306.clone.1..sunk.2, s32[]{:T(128)S(6)} %select_n.185) | dynamic-update-slice | bytes 1056788 | tf_op jit(solution)/shard_map/while/body/dynamic_update_slice | solution.py:154
  221.5 6.1 slice.174
  227.6 105.8 %collective-permute-start.1 = (f32[256,2,2048]{2,1,0:T(2,128)}, f32[256,2,2048]{2,1,0:T(2,128)}, u32[]{:S(2)}, u32[]{:S(2)}) collective-permute-start(f32[256,2,2048]{2,1,0:T(2,128)} %slice.174), channel_id=1, source_target_pairs={{0,1},{1,2},{2,3},{3,4},{4,5},{5,6},{6,7},{7,8},{8,9},{9,10},{10,1... | collective-permute-start | bytes 12582920 | tf_op jit(solution)/shard_map/ppermute | solution.py:11
  334.0 456.0 %collective-permute-done.1 = f32[256,2,2048]{2,1,0:T(2,128)} collective-permute-done((f32[256,2,2048]{2,1,0:T(2,128)}, f32[256,2,2048]{2,1,0:T(2,128)}, u32[]{:S(2)}, u32[]{:S(2)}) %collective-permute-start.1) | collective-permute-done | bytes 4194336 | tf_op jit(solution)/shard_map/ppermute | solution.py:11
  790.0 9.5 %slice_add_fusion = f32[256,2,2048]{2,1,0:T(2,128)} fusion(f32[256,2,2048]{2,1,0:T(2,128)} %collective-permute-done.1, f32[512,2,2048]{2,1,0:T(2,128)} %get-tuple-element.358), kind=kLoop, calls=%fused_computation.73 | loop fusion | flops 1048576 | bytes 12582912 | tf_op jit(solution)/shard_map/add | solution.py:165
  799.5 12.1 %reduce_sum.76 = f32[4,256,2,256]{3,1,2,0:T(8,128)S(1)} reduce(f32[16,4,256,2,256]{4,2,3,1,0:T(8,128)} %bitcast.178, f32[]{:T(128)} %constant.307.clone.1), dimensions={0}, to_apply=%region_14.15 | reduce | flops 7864320 | bytes 35651588 | tf_op jit(solution)/shard_map/reduce_sum | solution.py:146
  811.6 2.9 copy.48
  (92 shorter events, 42.2 us)
Async XLA Ops:
  7.2 792.3 %all-gather.3.cloned.1.call-start = ((), (), s32[]{:S(2)}) async-start(), calls=%async_computation | async-start | bytes 35651584 | tf_op jit(solution)/shard_map/all_gather | solution.py:146
  7.2 26.6 %collective-permute-start = (bf16[256,2,2048]{2,1,0:T(2,128)(2,1)}, bf16[256,2,2048]{2,1,0:T(2,128)(2,1)}, u32[]{:S(2)}, u32[]{:S(2)}) collective-permute-start(bf16[256,2,2048]{2,1,0:T(2,128)(2,1)} %param.21), channel_id=1, source_target_pairs={{1,0},{2,1},{3,2},{4,3},{5,4},{6,5},{7,6},{8,7},{9,8},{10,9},{11,1... | collective-permute-start | bytes 6291464 | tf_op jit(solution)/shard_map/ppermute | solution.py:11
  21.1 22.3 %copy-start.6 = (s32[6]{0:T(128)S(1)}, s32[6]{0:T(128)}, u32[]{:S(2)}) copy-start(s32[6]{0:T(128)} %param.24) | copy-start | bytes 76
  21.2 22.3 %copy-start.7 = (s32[6]{0:T(128)S(1)}, s32[6]{0:T(128)}, u32[]{:S(2)}) copy-start(s32[6]{0:T(128)} %param.25) | copy-start | bytes 76
  105.2 5.1 copy-start.5
  105.2 5.1 copy-start.8
  115.9 0.7 copy-start.3
  129.0 1.6 copy-start
  135.2 1.8 copy-start.4
  137.0 1.6 copy-start.1
  139.1 1.3 copy-start.2
  227.6 562.4 %collective-permute-start.1 = (f32[256,2,2048]{2,1,0:T(2,128)}, f32[256,2,2048]{2,1,0:T(2,128)}, u32[]{:S(2)}, u32[]{:S(2)}) collective-permute-start(f32[256,2,2048]{2,1,0:T(2,128)} %slice.174), channel_id=1, source_target_pairs={{0,1},{1,2},{2,3},{3,4},{4,5},{5,6},{6,7},{7,8},{8,9},{9,10},{10,1... | collective-permute-start | bytes 12582920 | tf_op jit(solution)/shard_map/ppermute | solution.py:11
Sparse Core Ops, SparseCore 0:
  145.6 380.8 all-gather.2
